TPU v7x, 256 devices: a whole 4x4x8 slice. The times are simulated.
256 devices in a mesh: prop: 8 (over x, core), dom: 32 (over z, y).
Axes of the slice: x: 4, y: 4, z: 8, core: 2. Of those that a mesh axis runs over, the one named last changes fastest.
Arguments:
- states: float32 [8, 128, 64, 128], P('prop', 'dom'), may hold values from -4 to 4
- accepted: int32 [1], replicated, may hold values from 0 to 7
- noise: float32 [8, 128, 64, 128], P('prop', 'dom'), may hold values from -5 to 5
- source: float32 [128, 64, 128], P('dom'), may hold values from -6 to 6
Outputs:
- pressure: float32 [8, 128, 64, 128], P('prop', 'dom')
All inputs are finite; a program needn't handle non-finite values.
Results may differ from a plain program's by a relative error of at most 0.0003.
Values sent between devices are 32-bit elements; how exact they have to be, the bound alone decides.
A program may use at most 128 MiB of HBM per device.

v0:
```python
import math
import jax
import jax.numpy as jnp
from jax import lax
from jax.sharding import PartitionSpec as P

LEVELS = 4
SWEEPS = 2
COARSE_SWEEPS = 64
OMEGA = 0.7
BETA = 0.4
SHRINK = math.sqrt(1.0 - BETA * BETA)
ZSCALE = 16.0


def padded_2(x, sides, width):
    for axis, dim in sides:
        devices, length = (lax.axis_size(axis), x.shape[dim])
        up = [(i, (i + 1) % devices) for i in range(devices - 1)]
        down = [(j, i) for i, j in up]
        last = lax.slice_in_dim(x, length - width, length, axis=dim)
        initial = lax.slice_in_dim(x, 0, width, axis=dim)
        before = lax.ppermute(last, axis, up)
        after = lax.ppermute(initial, axis, down)
        x = jnp.concatenate([before, x, after], axis=dim)
    return x


def from_root(x, axis, root):
    mine = lax.axis_index(axis) == root
    return lax.psum(jnp.where(mine, x, jnp.zeros_like(x)), axis)


def shift_lower(values, axis):
    axis = values.ndim + axis
    count = values.shape[axis]
    kept = lax.slice_in_dim(values, 0, count - 1, axis=axis)
    return jnp.concatenate(
        [jnp.zeros_like(lax.slice_in_dim(values, 0, 1, axis=axis)), kept], axis=axis
    )


def shift_upper(values, axis):
    axis = values.ndim + axis
    count = values.shape[axis]
    kept = lax.slice_in_dim(values, 1, count, axis=axis)
    return jnp.concatenate(
        [kept, jnp.zeros_like(lax.slice_in_dim(values, 0, 1, axis=axis))], axis=axis
    )


def harmonic(first, second):
    return 2.0 * first * second / (first + second)


def coefficients(perm, padded, scale):
    inner_x = harmonic(perm[..., 1:, :], perm[..., :-1, :])
    west = jnp.concatenate([perm[..., :1, :], inner_x], axis=-2)
    east = jnp.concatenate([inner_x, perm[..., -1:, :]], axis=-2)
    inner_y = harmonic(perm[..., 1:], perm[..., :-1])
    south = jnp.concatenate([perm[..., :1], inner_y], axis=-1)
    north = jnp.concatenate([inner_y, perm[..., -1:]], axis=-1)
    below = harmonic(padded[..., :-2, :, :], perm)
    above = harmonic(padded[..., 2:, :, :], perm)
    zfactor = ZSCALE * scale
    parts = [
        west * scale,
        east * scale,
        south * scale,
        north * scale,
        below * zfactor,
        above * zfactor,
    ]
    diagonal = parts[0] + parts[1] + parts[2] + parts[3] + parts[4] + parts[5]
    return parts + [diagonal, OMEGA / diagonal]


def apply_op(values, padded, coefs):
    result = (
        coefs[6] * values - coefs[0] * shift_lower(values, -2) - coefs[1] * shift_upper(values, -2)
    )
    result = result - coefs[2] * shift_lower(values, -1) - coefs[3] * shift_upper(values, -1)
    return result - coefs[4] * padded[..., :-2, :, :] - coefs[5] * padded[..., 2:, :, :]


def sweep(values, right, coefs, pad_z):
    return values + coefs[7] * (right - apply_op(values, pad_z(values), coefs))


def sum_children(values):
    shape = values.shape
    split = values.reshape(shape[:-3] + (shape[-3] // 2, 2, shape[-2] // 2, 2, shape[-1] // 2, 2))
    return split.sum(axis=(-5, -3, -1))


def prolong(values):
    return jnp.repeat(jnp.repeat(jnp.repeat(values, 2, axis=-3), 2, axis=-2), 2, axis=-1)


def zero_pad(values):
    widths = [(0, 0)] * (values.ndim - 3) + [(1, 1), (0, 0), (0, 0)]
    return jnp.pad(values, widths)


def pressure_rim(values):
    return padded_2(values, (("dom", 1),), 1)


def perm_rim(values):
    return padded_2(values, (("dom", 1),), 1)


def coarse_solve(right, perm, level, pad_z, pad_perm):
    coefs = coefficients(perm, pad_perm(perm), 4.0**level)
    start = coefs[7] * right
    return lax.fori_loop(
        0, COARSE_SWEEPS - 1, lambda step, values: sweep(values, right, coefs, pad_z), start
    )


def level_cycle(right, perm, level, pad_z, pad_perm, deeper):
    coefs = coefficients(perm, pad_perm(perm), 4.0**level)
    values = coefs[7] * right
    values = sweep(values, right, coefs, pad_z)
    residue = right - apply_op(values, pad_z(values), coefs)
    update = deeper(sum_children(residue), sum_children(perm) * 0.125, level + 1)
    values = values + prolong(update)
    for step in range(SWEEPS):
        values = sweep(values, right, coefs, pad_z)
    return values


def local_cycle(right, perm, level):
    if level == LEVELS - 1:
        return coarse_solve(right, perm, level, zero_pad, zero_pad)
    return level_cycle(right, perm, level, zero_pad, zero_pad, local_cycle)


def body(states, accepted, noise, source):
    per_device = states.shape[0]
    chosen = accepted[0]
    owner = chosen // per_device
    picked = lax.dynamic_index_in_dim(states, chosen % per_device, 0, keepdims=False)
    current = from_root(picked, "prop", owner)
    theta = SHRINK * current[None] + BETA * noise
    perm = jnp.exp(theta)
    right = source[None]
    gather_level = 2

    def spread_cycle(right_side, field, level):
        if level == gather_level:
            whole_right, whole_perm = (
                lax.all_gather(right_side, "dom", axis=1, tiled=True),
                lax.all_gather(field, "dom", axis=1, tiled=True),
            )
            result = local_cycle(whole_right, whole_perm, level)
            height = right_side.shape[1]
            return lax.dynamic_slice_in_dim(result, lax.axis_index("dom") * height, height, 1)
        return level_cycle(right_side, field, level, pressure_rim, perm_rim, spread_cycle)

    return spread_cycle(right, perm, 0)


def solution(mesh):
    in_specs = (
        P("prop", "dom", None, None),
        P(),
        P("prop", "dom", None, None),
        P("dom", None, None),
    )
    out_specs = P("prop", "dom", None, None)
    return jax.shard_map(body, mesh=mesh, in_specs=in_specs, out_specs=out_specs, check_vma=False)
```

profile of v0, /device:TPU:120, one launch (start us, length us, event | category | flops | bytes accessed | tf_op | source)
XLA Modules:
  0.0 459.8 jit_solution(12875724920466572557)
XLA Ops:
  11.1 65.1 %all-reduce.61.cloned.1.call-done = f32[4,64,128]{1,2,0:T(8,128)} async-done(((f32[4,64,128]{1,2,0:T(8,128)}), f32[4,64,128]{1,2,0:T(8,128)}) %all-reduce.61.cloned.1.call-update) | async-done | bytes 131088 | tf_op jit(solution)/shard_map/psum | solution.py:31
  78.3 9.8 %reshape.767 = f32[2,2,32,2,64,2]{5,4,3,2,1,0:T(8,128)} reshape(f32[1,4,64,128]{3,2,1,0:T(8,128)S(1)} %copy.50) | data formatting | bytes 262144 | tf_op jit(solution)/shard_map/reshape | solution.py:92
  88.1 4.0 reduce_sum.74
  94.8 48.6 %all-gather = f32[512,32]{1,0:T(8,128)S(1)} all-gather(f32[16,32]{1,0:T(8,128)S(1)} %broadcast_multiply_fusion), channel_id=2, replica_groups=mesh['prop'=8,'dom'=32] {'dom'}, dimensions={0}, use_global_device_ids=true | all-gather | bytes 67584 | tf_op jit(solution)/shard_map/all_gather | solution.py:154
  145.8 5.5 %reshape.769 = f32[16,2,8,2,16,2]{3,2,1,0,5,4:T(8,128)} reshape(f32[512,32]{0,1:T(8,128)S(1)} %copy.52) | data formatting | bytes 131072 | tf_op jit(solution)/shard_map/reshape | solution.py:92
  151.4 2.6 reduce_sum.84
  154.2 4.6 collective-permute-start
  158.8 1.9 collective-permute-start.1
  160.8 7.2 %collective-permute-start.4 = (f32[1,1,32,64]{3,2,1,0:T(8,128)}, f32[1,1,32,64]{3,2,1,0:T(8,128)S(1)}, u32[]{:S(2)}, u32[]{:S(2)}) collective-permute-start(f32[1,1,32,64]{3,2,1,0:T(8,128)} %get-tuple-element.298), channel_id=1, source_target_pairs={{0,1},{1,2},{2,3},{3,4},{4,5},{5,6},{6,7},{7,8},{8,9},{9,10},{10,1... | collective-permute-start | bytes 24584 | tf_op jit(solution)/shard_map/ppermute | solution.py:23
  168.0 1.9 collective-permute-start.5
  171.5 1.6 copy.56
  173.2 1.6 copy.57
  179.0 7.2 %collective-permute-start.2 = (f32[1,1,64,128]{2,3,1,0:T(8,128)S(1)}, f32[1,1,64,128]{2,3,1,0:T(8,128)S(1)}, u32[]{:S(2)}, u32[]{:S(2)}) collective-permute-start(f32[1,1,64,128]{2,3,1,0:T(8,128)S(1)} %get-tuple-element.255), channel_id=1, source_target_pairs={{0,1},{1,2},{2,3},{3,4},{4,5},{5,6},{6,7},{7,8},{8,9},{9,10},{10,1... | collective-permute-start | bytes 98312 | tf_op jit(solution)/shard_map/ppermute | solution.py:23
  186.2 1.9 collective-permute-start.3
  188.2 7.5 %collective-permute-done.3 = f32[1,1,64,128]{2,3,1,0:T(8,128)S(1)} collective-permute-done((f32[1,1,64,128]{2,3,1,0:T(8,128)S(1)}, f32[1,1,64,128]{2,3,1,0:T(8,128)S(1)}, u32[]{:S(2)}, u32[]{:S(2)}) %collective-permute-start.3) | collective-permute-done | bytes 32800 | tf_op jit(solution)/shard_map/ppermute | solution.py:24
  196.3 1.9 collective-permute-start.6
  198.2 3.9 collective-permute-start.7
  202.4 5.2 %collective-permute-done.7 = f32[1,1,64,128]{2,3,1,0:T(8,128)S(1)} collective-permute-done((f32[1,1,64,128]{2,3,1,0:T(8,128)S(1)}, f32[1,1,64,128]{2,3,1,0:T(8,128)S(1)}, u32[]{:S(2)}, u32[]{:S(2)}) %collective-permute-start.7) | collective-permute-done | bytes 32800 | tf_op jit(solution)/shard_map/ppermute | solution.py:24
  208.2 9.8 %reshape.768 = f32[2,2,32,2,64,2]{5,4,3,2,1,0:T(8,128)} reshape(f32[1,4,64,128]{3,2,1,0:T(8,128)S(1)} %copy.51) | data formatting | bytes 262144 | tf_op jit(solution)/shard_map/reshape | solution.py:92
  218.0 4.0 reduce_sum.75
  222.3 1.9 collective-permute-start.8
  224.2 3.9 collective-permute-start.9
  228.2 4.9 %collective-permute-done.9 = f32[1,1,32,64]{3,2,1,0:T(8,128)S(1)} collective-permute-done((f32[1,1,32,64]{3,2,1,0:T(8,128)S(1)}, f32[1,1,32,64]{3,2,1,0:T(8,128)S(1)}, u32[]{:S(2)}, u32[]{:S(2)}) %collective-permute-start.9) | collective-permute-done | bytes 8224 | tf_op jit(solution)/shard_map/ppermute | solution.py:24
  233.3 1.9 collective-permute-start.10
  235.2 3.9 collective-permute-start.11
  239.2 4.9 %collective-permute-done.11 = f32[1,1,32,64]{3,2,1,0:T(8,128)S(1)} collective-permute-done((f32[1,1,32,64]{3,2,1,0:T(8,128)S(1)}, f32[1,1,32,64]{3,2,1,0:T(8,128)S(1)}, u32[]{:S(2)}, u32[]{:S(2)}) %collective-permute-start.11) | collective-permute-done | bytes 8224 | tf_op jit(solution)/shard_map/ppermute | solution.py:24
  245.0 46.0 %all-gather.1 = f32[512,32]{1,0:T(8,128)S(1)} all-gather(f32[16,32]{1,0:T(8,128)S(1)} %reduce_sum.82), channel_id=3, replica_groups=mesh['prop'=8,'dom'=32] {'dom'}, dimensions={0}, use_global_device_ids=true | all-gather | bytes 67584 | tf_op jit(solution)/shard_map/all_gather | solution.py:153
  291.0 1.6 fusion.107
  294.0 1.8 fusion.17
  295.8 4.5 reshape.770
  300.3 2.5 reduce_sum.85
  303.6 1.6 bitcast_multiply_fusion.2
  306.3 1.6 copy.62
  307.9 84.0 %while.15 = (s32[]{:T(128)}, f32[1,16,8,16]{3,2,1,0:T(8,128)S(1)}, f32[1,16,8,16]{3,2,1,0:T(8,128)}, f32[1,16,8,16]{3,2,1,0:T(8,128)}, f32[1,16,8,16]{3,2,1,0:T(...) while((s32[]{:T(128)}, f32[1,16,8,16]{3,2,1,0:T(8,128)S(1)}, ...), condition=%wide.region_10.11_spmd, body=%wide.region_9.10_spmd.sunk | while | flops 32770 | bytes 195701 | solution.py:116
  309.4 1.2 fusion.158
  312.0 1.2 fusion.158
  314.7 1.2 fusion.158
  317.4 1.2 fusion.158
  332.0 1.2 fusion.158
  334.7 1.2 fusion.158
  337.4 1.2 fusion.158
  340.0 1.2 fusion.158
  342.7 1.2 fusion.158
  357.4 1.2 fusion.158
  360.1 1.2 fusion.158
  362.7 1.2 fusion.158
  365.4 1.2 fusion.158
  368.1 1.2 fusion.158
  382.7 1.2 fusion.158
  385.4 1.2 fusion.158
  394.4 1.8 copy.65
  397.4 1.3 fusion.24
  400.2 4.6 collective-permute-start.12
  404.8 1.9 collective-permute-start.13
  406.8 7.0 %collective-permute-done.13 = f32[1,1,32,64]{3,2,1,0:T(8,128)S(1)} collective-permute-done((f32[1,1,32,64]{3,2,1,0:T(8,128)S(1)}, f32[1,1,32,64]{3,2,1,0:T(8,128)S(1)}, u32[]{:S(2)}, u32[]{:S(2)}) %collective-permute-start.13) | collective-permute-done | bytes 8224 | tf_op jit(solution)/shard_map/ppermute | solution.py:24
  414.7 1.9 collective-permute-start.14
  416.7 3.9 collective-permute-start.15
  420.7 4.9 %collective-permute-done.15 = f32[1,1,32,64]{3,2,1,0:T(8,128)S(1)} collective-permute-done((f32[1,1,32,64]{3,2,1,0:T(8,128)S(1)}, f32[1,1,32,64]{3,2,1,0:T(8,128)S(1)}, u32[]{:S(2)}, u32[]{:S(2)}) %collective-permute-start.15) | collective-permute-done | bytes 8224 | tf_op jit(solution)/shard_map/ppermute | solution.py:24
  426.9 1.9 collective-permute-start.16
  428.8 3.9 collective-permute-start.17
  433.1 5.2 %collective-permute-done.17 = f32[1,1,64,128]{2,3,1,0:T(8,128)S(1)} collective-permute-done((f32[1,1,64,128]{2,3,1,0:T(8,128)S(1)}, f32[1,1,64,128]{2,3,1,0:T(8,128)S(1)}, u32[]{:S(2)}, u32[]{:S(2)}) %collective-permute-start.17) | collective-permute-done | bytes 32800 | tf_op jit(solution)/shard_map/ppermute | solution.py:24
  439.6 1.9 collective-permute-start.18
  441.5 3.9 collective-permute-start.19
  445.8 5.2 %collective-permute-done.19 = f32[1,1,64,128]{2,3,1,0:T(8,128)S(1)} collective-permute-done((f32[1,1,64,128]{2,3,1,0:T(8,128)S(1)}, f32[1,1,64,128]{2,3,1,0:T(8,128)S(1)}, u32[]{:S(2)}, u32[]{:S(2)}) %collective-permute-start.19) | collective-permute-done | bytes 32800 | tf_op jit(solution)/shard_map/ppermute | solution.py:24
  (397 shorter events, 96.6 us)
Async XLA Ops:
  6.5 69.6 %all-reduce.61.cloned.1.call-start = ((), (), s32[]{:S(2)}) async-start(), calls=%async_computation | async-start | bytes 524288 | tf_op jit(solution)/shard_map/psum | solution.py:31
  77.8 129.9 %copy-start.18 = (f32[1,4,64,1]{2,3,1,0:T(1,128)}, f32[1,4,64,1]{2,3,1,0:T(1,128)S(1)}, u32[]{:S(2)}) copy-start(f32[1,4,64,1]{2,3,1,0:T(1,128)S(1)} %get-tuple-element.261) | copy-start | bytes 3076
  77.8 129.9 %copy-start.19 = (f32[1,4,64,1]{2,3,1,0:T(1,128)}, f32[1,4,64,1]{2,3,1,0:T(1,128)S(1)}, u32[]{:S(2)}) copy-start(f32[1,4,64,1]{2,3,1,0:T(1,128)S(1)} %get-tuple-element.262) | copy-start | bytes 3076
  93.3 150.8 %copy-start.8 = (f32[1,2,31,64]{3,2,1,0:T(8,128)}, f32[1,2,31,64]{3,2,1,0:T(8,128)S(1)}, u32[]{:S(2)}) copy-start(f32[1,2,31,64]{3,2,1,0:T(8,128)S(1)} %add_divide_fusion.7) | copy-start | bytes 47620
  154.2 24.2 %collective-permute-start = (f32[1,1,64,128]{2,3,1,0:T(8,128)}, f32[1,1,64,128]{2,3,1,0:T(8,128)S(1)}, u32[]{:S(2)}, u32[]{:S(2)}) collective-permute-start(f32[1,1,64,128]{2,3,1,0:T(8,128)} %get-tuple-element.260), channel_id=1, source_target_pairs={{0,1},{1,2},{2,3},{3,4},{4,5},{5,6},{6,7},{7,8},{8,9},{9,10},{10,1... | collective-permute-start | bytes 98312 | tf_op jit(solution)/shard_map/ppermute | solution.py:23
  158.8 19.6 %collective-permute-start.1 = (f32[1,1,64,128]{2,3,1,0:T(8,128)}, f32[1,1,64,128]{2,3,1,0:T(8,128)S(1)}, u32[]{:S(2)}, u32[]{:S(2)}) collective-permute-start(f32[1,1,64,128]{2,3,1,0:T(8,128)} %get-tuple-element.259), channel_id=1, source_target_pairs={{1,0},{2,1},{3,2},{4,3},{5,4},{6,5},{7,6},{8,7},{9,8},{10,9},{11,1... | collective-permute-start | bytes 98312 | tf_op jit(solution)/shard_map/ppermute | solution.py:24
  160.8 61.3 %collective-permute-start.4 = (f32[1,1,32,64]{3,2,1,0:T(8,128)}, f32[1,1,32,64]{3,2,1,0:T(8,128)S(1)}, u32[]{:S(2)}, u32[]{:S(2)}) collective-permute-start(f32[1,1,32,64]{3,2,1,0:T(8,128)} %get-tuple-element.298), channel_id=1, source_target_pairs={{0,1},{1,2},{2,3},{3,4},{4,5},{5,6},{6,7},{7,8},{8,9},{9,10},{10,1... | collective-permute-start | bytes 24584 | tf_op jit(solution)/shard_map/ppermute | solution.py:23
  168.0 54.1 %collective-permute-start.5 = (f32[1,1,32,64]{3,2,1,0:T(8,128)}, f32[1,1,32,64]{3,2,1,0:T(8,128)S(1)}, u32[]{:S(2)}, u32[]{:S(2)}) collective-permute-start(f32[1,1,32,64]{3,2,1,0:T(8,128)} %get-tuple-element.297), channel_id=1, source_target_pairs={{1,0},{2,1},{3,2},{4,3},{5,4},{6,5},{7,6},{8,7},{9,8},{10,9},{11,1... | collective-permute-start | bytes 24584 | tf_op jit(solution)/shard_map/ppermute | solution.py:24
  170.8 24.9 %copy-start.7 = (f32[1,16,8,16]{2,1,3,0:T(8,128)}, f32[1,16,8,16]{2,1,3,0:T(8,128)S(1)}, u32[]{:S(2)}) copy-start(f32[1,16,8,16]{2,1,3,0:T(8,128)S(1)} %get-tuple-element.188) | copy-start | bytes 24580
  178.5 39.6 %copy-start.1 = (f32[1,1,64,128]{2,3,1,0:T(8,128)}, f32[1,1,64,128]{2,3,1,0:T(8,128)S(1)}, u32[]{:S(2)}) copy-start(f32[1,1,64,128]{2,3,1,0:T(8,128)S(1)} %collective-permute-done) | copy-start | bytes 98308
  178.5 39.6 %copy-start.3 = (f32[1,1,64,128]{2,3,1,0:T(8,128)}, f32[1,1,64,128]{2,3,1,0:T(8,128)S(1)}, u32[]{:S(2)}) copy-start(f32[1,1,64,128]{2,3,1,0:T(8,128)S(1)} %collective-permute-done.1) | copy-start | bytes 98308
  179.0 9.2 %collective-permute-start.2 = (f32[1,1,64,128]{2,3,1,0:T(8,128)S(1)}, f32[1,1,64,128]{2,3,1,0:T(8,128)S(1)}, u32[]{:S(2)}, u32[]{:S(2)}) collective-permute-start(f32[1,1,64,128]{2,3,1,0:T(8,128)S(1)} %get-tuple-element.255), channel_id=1, source_target_pairs={{0,1},{1,2},{2,3},{3,4},{4,5},{5,6},{6,7},{7,8},{8,9},{9,10},{10,1... | collective-permute-start | bytes 98312 | tf_op jit(solution)/shard_map/ppermute | solution.py:23
  186.2 9.5 %collective-permute-start.3 = (f32[1,1,64,128]{2,3,1,0:T(8,128)S(1)}, f32[1,1,64,128]{2,3,1,0:T(8,128)S(1)}, u32[]{:S(2)}, u32[]{:S(2)}) collective-permute-start(f32[1,1,64,128]{2,3,1,0:T(8,128)S(1)} %get-tuple-element.256), channel_id=1, source_target_pairs={{1,0},{2,1},{3,2},{4,3},{5,4},{6,5},{7,6},{8,7},{9,8},{10,9},{11,1... | collective-permute-start | bytes 98312 | tf_op jit(solution)/shard_map/ppermute | solution.py:24
  196.3 6.2 %collective-permute-start.6 = (f32[1,1,64,128]{2,3,1,0:T(8,128)S(1)}, f32[1,1,64,128]{2,3,1,0:T(8,128)S(1)}, u32[]{:S(2)}, u32[]{:S(2)}) collective-permute-start(f32[1,1,64,128]{2,3,1,0:T(8,128)S(1)} %get-tuple-element.249), channel_id=1, source_target_pairs={{0,1},{1,2},{2,3},{3,4},{4,5},{5,6},{6,7},{7,8},{8,9},{9,10},{10,1... | collective-permute-start | bytes 98312 | tf_op jit(solution)/shard_map/ppermute | solution.py:23
  198.2 9.5 %collective-permute-start.7 = (f32[1,1,64,128]{2,3,1,0:T(8,128)S(1)}, f32[1,1,64,128]{2,3,1,0:T(8,128)S(1)}, u32[]{:S(2)}, u32[]{:S(2)}) collective-permute-start(f32[1,1,64,128]{2,3,1,0:T(8,128)S(1)} %get-tuple-element.250), channel_id=1, source_target_pairs={{1,0},{2,1},{3,2},{4,3},{5,4},{6,5},{7,6},{8,7},{9,8},{10,9},{11,1... | collective-permute-start | bytes 98312 | tf_op jit(solution)/shard_map/ppermute | solution.py:24
  208.2 13.9 %copy-start.17 = (f32[1,2,32,1]{3,2,1,0:T(8,128)S(1)}, f32[1,2,32,1]{3,2,1,0:T(8,128)}, u32[]{:S(2)}) copy-start(f32[1,2,32,1]{3,2,1,0:T(8,128)} %get-tuple-element.296) | copy-start | bytes 772
  208.2 13.9 %copy-start.20 = (f32[1,2,1,64]{3,2,1,0:T(1,128)S(1)}, f32[1,2,1,64]{3,2,1,0:T(1,128)}, u32[]{:S(2)}) copy-start(f32[1,2,1,64]{3,2,1,0:T(1,128)} %get-tuple-element.299) | copy-start | bytes 1540
  208.2 13.9 %copy-start.21 = (f32[1,2,1,64]{3,2,1,0:T(1,128)S(1)}, f32[1,2,1,64]{3,2,1,0:T(1,128)}, u32[]{:S(2)}) copy-start(f32[1,2,1,64]{3,2,1,0:T(1,128)} %get-tuple-element.300) | copy-start | bytes 1540
  222.0 73.8 %copy-start.5 = (f32[2,32,64]{2,1,0:T(8,128)}, f32[2,32,64]{2,1,0:T(8,128)S(1)}, u32[]{:S(2)}) copy-start(f32[2,32,64]{2,1,0:T(8,128)S(1)} %reduce_sum.75) | copy-start | bytes 49156
  222.1 22.1 %copy-start.15 = (f32[1,1,32,64]{3,2,1,0:T(8,128)}, f32[1,1,32,64]{3,2,1,0:T(8,128)S(1)}, u32[]{:S(2)}) copy-start(f32[1,1,32,64]{3,2,1,0:T(8,128)S(1)} %collective-permute-done.4) | copy-start | bytes 24580
  222.1 22.1 %copy-start.16 = (f32[1,1,32,64]{3,2,1,0:T(8,128)}, f32[1,1,32,64]{3,2,1,0:T(8,128)S(1)}, u32[]{:S(2)}) copy-start(f32[1,1,32,64]{3,2,1,0:T(8,128)S(1)} %collective-permute-done.5) | copy-start | bytes 24580
  222.2 21.9 %copy-start.10 = (f32[1,2,32,64]{3,2,1,0:T(8,128)}, f32[1,2,32,64]{3,2,1,0:T(8,128)S(1)}, u32[]{:S(2)}) copy-start(f32[1,2,32,64]{3,2,1,0:T(8,128)S(1)} %get-tuple-element.200) | copy-start | bytes 49156
  222.2 21.9 %copy-start.12 = (f32[1,2,32,64]{3,2,1,0:T(8,128)}, f32[1,2,32,64]{3,2,1,0:T(8,128)S(1)}, u32[]{:S(2)}) copy-start(f32[1,2,32,64]{3,2,1,0:T(8,128)S(1)} %get-tuple-element.201) | copy-start | bytes 49156
  222.3 5.9 %collective-permute-start.8 = (f32[1,1,32,64]{3,2,1,0:T(8,128)S(1)}, f32[1,1,32,64]{3,2,1,0:T(8,128)S(1)}, u32[]{:S(2)}, u32[]{:S(2)}) collective-permute-start(f32[1,1,32,64]{3,2,1,0:T(8,128)S(1)} %get-tuple-element.293), channel_id=1, source_target_pairs={{0,1},{1,2},{2,3},{3,4},{4,5},{5,6},{6,7},{7,8},{8,9},{9,10},{10,1... | collective-permute-start | bytes 24584 | tf_op jit(solution)/shard_map/ppermute | solution.py:23
  224.2 9.0 %collective-permute-start.9 = (f32[1,1,32,64]{3,2,1,0:T(8,128)S(1)}, f32[1,1,32,64]{3,2,1,0:T(8,128)S(1)}, u32[]{:S(2)}, u32[]{:S(2)}) collective-permute-start(f32[1,1,32,64]{3,2,1,0:T(8,128)S(1)} %get-tuple-element.294), channel_id=1, source_target_pairs={{1,0},{2,1},{3,2},{4,3},{5,4},{6,5},{7,6},{8,7},{9,8},{10,9},{11,1... | collective-permute-start | bytes 24584 | tf_op jit(solution)/shard_map/ppermute | solution.py:24
  233.3 5.9 %collective-permute-start.10 = (f32[1,1,32,64]{3,2,1,0:T(8,128)S(1)}, f32[1,1,32,64]{3,2,1,0:T(8,128)S(1)}, u32[]{:S(2)}, u32[]{:S(2)}) collective-permute-start(f32[1,1,32,64]{3,2,1,0:T(8,128)S(1)} %get-tuple-element.287), channel_id=1, source_target_pairs={{0,1},{1,2},{2,3},{3,4},{4,5},{5,6},{6,7},{7,8},{8,9},{9,10},{10,1... | collective-permute-start | bytes 24584 | tf_op jit(solution)/shard_map/ppermute | solution.py:23
  235.2 9.0 %collective-permute-start.11 = (f32[1,1,32,64]{3,2,1,0:T(8,128)S(1)}, f32[1,1,32,64]{3,2,1,0:T(8,128)S(1)}, u32[]{:S(2)}, u32[]{:S(2)}) collective-permute-start(f32[1,1,32,64]{3,2,1,0:T(8,128)S(1)} %get-tuple-element.288), channel_id=1, source_target_pairs={{1,0},{2,1},{3,2},{4,3},{5,4},{6,5},{7,6},{8,7},{9,8},{10,9},{11,1... | collective-permute-start | bytes 24584 | tf_op jit(solution)/shard_map/ppermute | solution.py:24
  292.6 1.3 copy-start
  396.2 2.8 copy-start.14
  397.2 16.7 %copy-start.6 = (f32[2,32,64]{2,1,0:T(8,128)S(1)}, f32[2,32,64]{2,1,0:T(8,128)}, u32[]{:S(2)}) copy-start(f32[2,32,64]{2,1,0:T(8,128)} %copy-done.5) | copy-start | bytes 49156
  397.2 16.6 %copy-start.9 = (f32[1,2,31,64]{3,2,1,0:T(8,128)S(1)}, f32[1,2,31,64]{3,2,1,0:T(8,128)}, u32[]{:S(2)}) copy-start(f32[1,2,31,64]{3,2,1,0:T(8,128)} %copy-done.8) | copy-start | bytes 47620
  397.2 16.6 %copy-start.11 = (f32[1,2,32,64]{3,2,1,0:T(8,128)S(1)}, f32[1,2,32,64]{3,2,1,0:T(8,128)}, u32[]{:S(2)}) copy-start(f32[1,2,32,64]{3,2,1,0:T(8,128)} %copy-done.10) | copy-start | bytes 49156
  397.2 16.6 %copy-start.13 = (f32[1,2,32,64]{3,2,1,0:T(8,128)S(1)}, f32[1,2,32,64]{3,2,1,0:T(8,128)}, u32[]{:S(2)}) copy-start(f32[1,2,32,64]{3,2,1,0:T(8,128)} %copy-done.12) | copy-start | bytes 49156
  397.3 41.0 %copy-start.2 = (f32[1,1,64,128]{2,3,1,0:T(8,128)S(1)}, f32[1,1,64,128]{2,3,1,0:T(8,128)}, u32[]{:S(2)}) copy-start(f32[1,1,64,128]{2,3,1,0:T(8,128)} %copy-done.1) | copy-start | bytes 98308
  397.3 41.0 %copy-start.4 = (f32[1,1,64,128]{2,3,1,0:T(8,128)S(1)}, f32[1,1,64,128]{2,3,1,0:T(8,128)}, u32[]{:S(2)}) copy-start(f32[1,1,64,128]{2,3,1,0:T(8,128)} %copy-done.3) | copy-start | bytes 98308
  400.2 6.6 %collective-permute-start.12 = (f32[1,1,32,64]{3,2,1,0:T(8,128)S(1)}, f32[1,1,32,64]{3,2,1,0:T(8,128)S(1)}, u32[]{:S(2)}, u32[]{:S(2)}) collective-permute-start(f32[1,1,32,64]{3,2,1,0:T(8,128)S(1)} %get-tuple-element.279), channel_id=1, source_target_pairs={{0,1},{1,2},{2,3},{3,4},{4,5},{5,6},{6,7},{7,8},{8,9},{9,10},{10,1... | collective-permute-start | bytes 24584 | tf_op jit(solution)/shard_map/ppermute | solution.py:23
  404.8 9.0 %collective-permute-start.13 = (f32[1,1,32,64]{3,2,1,0:T(8,128)S(1)}, f32[1,1,32,64]{3,2,1,0:T(8,128)S(1)}, u32[]{:S(2)}, u32[]{:S(2)}) collective-permute-start(f32[1,1,32,64]{3,2,1,0:T(8,128)S(1)} %get-tuple-element.280), channel_id=1, source_target_pairs={{1,0},{2,1},{3,2},{4,3},{5,4},{6,5},{7,6},{8,7},{9,8},{10,9},{11,1... | collective-permute-start | bytes 24584 | tf_op jit(solution)/shard_map/ppermute | solution.py:24
  414.7 5.9 %collective-permute-start.14 = (f32[1,1,32,64]{3,2,1,0:T(8,128)S(1)}, f32[1,1,32,64]{3,2,1,0:T(8,128)S(1)}, u32[]{:S(2)}, u32[]{:S(2)}) collective-permute-start(f32[1,1,32,64]{3,2,1,0:T(8,128)S(1)} %get-tuple-element.273), channel_id=1, source_target_pairs={{0,1},{1,2},{2,3},{3,4},{4,5},{5,6},{6,7},{7,8},{8,9},{9,10},{10,1... | collective-permute-start | bytes 24584 | tf_op jit(solution)/shard_map/ppermute | solution.py:23
  416.7 9.0 %collective-permute-start.15 = (f32[1,1,32,64]{3,2,1,0:T(8,128)S(1)}, f32[1,1,32,64]{3,2,1,0:T(8,128)S(1)}, u32[]{:S(2)}, u32[]{:S(2)}) collective-permute-start(f32[1,1,32,64]{3,2,1,0:T(8,128)S(1)} %get-tuple-element.274), channel_id=1, source_target_pairs={{1,0},{2,1},{3,2},{4,3},{5,4},{6,5},{7,6},{8,7},{9,8},{10,9},{11,1... | collective-permute-start | bytes 24584 | tf_op jit(solution)/shard_map/ppermute | solution.py:24
  426.9 6.2 %collective-permute-start.16 = (f32[1,1,64,128]{2,3,1,0:T(8,128)S(1)}, f32[1,1,64,128]{2,3,1,0:T(8,128)S(1)}, u32[]{:S(2)}, u32[]{:S(2)}) collective-permute-start(f32[1,1,64,128]{2,3,1,0:T(8,128)S(1)} %get-tuple-element.219), channel_id=1, source_target_pairs={{0,1},{1,2},{2,3},{3,4},{4,5},{5,6},{6,7},{7,8},{8,9},{9,10},{10,1... | collective-permute-start | bytes 98312 | tf_op jit(solution)/shard_map/ppermute | solution.py:23
  428.8 9.5 %collective-permute-start.17 = (f32[1,1,64,128]{2,3,1,0:T(8,128)S(1)}, f32[1,1,64,128]{2,3,1,0:T(8,128)S(1)}, u32[]{:S(2)}, u32[]{:S(2)}) collective-permute-start(f32[1,1,64,128]{2,3,1,0:T(8,128)S(1)} %get-tuple-element.220), channel_id=1, source_target_pairs={{1,0},{2,1},{3,2},{4,3},{5,4},{6,5},{7,6},{8,7},{9,8},{10,9},{11,1... | collective-permute-start | bytes 98312 | tf_op jit(solution)/shard_map/ppermute | solution.py:24
  439.6 6.2 %collective-permute-start.18 = (f32[1,1,64,128]{2,3,1,0:T(8,128)S(1)}, f32[1,1,64,128]{2,3,1,0:T(8,128)S(1)}, u32[]{:S(2)}, u32[]{:S(2)}) collective-permute-start(f32[1,1,64,128]{2,3,1,0:T(8,128)S(1)} %get-tuple-element.213), channel_id=1, source_target_pairs={{0,1},{1,2},{2,3},{3,4},{4,5},{5,6},{6,7},{7,8},{8,9},{9,10},{10,1... | collective-permute-start | bytes 98312 | tf_op jit(solution)/shard_map/ppermute | solution.py:23
  441.5 9.5 %collective-permute-start.19 = (f32[1,1,64,128]{2,3,1,0:T(8,128)S(1)}, f32[1,1,64,128]{2,3,1,0:T(8,128)S(1)}, u32[]{:S(2)}, u32[]{:S(2)}) collective-permute-start(f32[1,1,64,128]{2,3,1,0:T(8,128)S(1)} %get-tuple-element.214), channel_id=1, source_target_pairs={{1,0},{2,1},{3,2},{4,3},{5,4},{6,5},{7,6},{8,7},{9,8},{10,9},{11,1... | collective-permute-start | bytes 98312 | tf_op jit(solution)/shard_map/ppermute | solution.py:24
Sparse Core Ops, SparseCore 0:
  9.7 66.4 all-reduce.60
where the time goes:
time: 465 us; the launch traced here: 460 us
  waiting for transfers between devices  111 us (24%)
  other arithmetic  108 us (23%)
  blocking collectives  94.6 us (20%)
  starting transfers between devices  66.4 us (14%)
  local copies, waits for them, and re-layouts  62.8 us (14%)
  between operations  15 us (3%)
    add x71, other arithmetic, sweep(): return values + coefs[7] * (right - apply_op(values, pad_z(values), coefs))  82.6 us
    psum x1, waiting for transfers between devices, from_root(): return lax.psum(jnp.where(mine, x, jnp.zeros_like(x)), axis)  65.1 us
    all_gather x1, blocking collectives, spread_cycle(): lax.all_gather(field, 'dom', axis=1, tiled=True)  48.6 us
    all_gather x1, blocking collectives, spread_cycle(): lax.all_gather(right_side, 'dom', axis=1, tiled=True)  46 us
    ppermute x10, waiting for transfers between devices, padded_2(): after = lax.ppermute(initial, axis, down)  45.1 us
    ppermute x10, starting transfers between devices, padded_2(): before = lax.ppermute(last, axis, up)  35.2 us
    ppermute x10, starting transfers between devices, padded_2(): after = lax.ppermute(initial, axis, down)  31.2 us
    reshape x4, local copies, waits for them, and re-layouts, sum_children(): values.reshape(shape[:-3] + (shape[-3] // 2, 2, shape[-2] // 2, 2, shape[...  29.6 us
  transfers between devices with their start and end apart: 21, of which 12 were waited for; matrix products, arithmetic and copies ran while one was open for 6% of the time, Pallas kernels for 0%

commit v1 on v0

--- a/solution.py
+++ b/solution.py
@@ -149,9 +149,18 @@
 
     def spread_cycle(right_side, field, level):
         if level == gather_level:
+            perform_the_strips_all = lambda arr_in: jnp.concatenate(
+                lax.all_to_all(
+                    jnp.stack([arr_in] * lax.axis_size("dom"), axis=0),
+                    "dom",
+                    split_axis=0,
+                    concat_axis=0,
+                ),
+                axis=1,
+            )
             whole_right, whole_perm = (
                 lax.all_gather(right_side, "dom", axis=1, tiled=True),
-                lax.all_gather(field, "dom", axis=1, tiled=True),
+                perform_the_strips_all(field),
             )
             result = local_cycle(whole_right, whole_perm, level)
             height = right_side.shape[1]

time: 465 us -> 412 us (0.89)
  blocking collectives: 94.6 us -> 46 us
  local copies, waits for them, and re-layouts: 62.8 us -> 49.6 us
  starting transfers between devices: 66.4 us -> 73.8 us
    all_gather x1 -> x0, blocking collectives: 48.6 us -> none  [spread_cycle(): lax.all_gather(field, 'dom', axis=1, tiled=True)]
    while x73 -> x63, local copies, waits for them, and re-layouts: 10.7 us -> 0.4 us  [the longest x10 10.3 us: coarse_solve(): lax.fori_loop(0, COARSE_SWEEPS - 1, lambda step, values: sweep(values, ri...]
    all_to_all x0 -> x1, starting transfers between devices: none -> 10.1 us  [spread_cycle(): lax.all_to_all(jnp.stack([arr_in] * lax.axis_size('dom'), axis=0), 'dom',...]
    reshape x4 -> x3, local copies, waits for them, and re-layouts: 29.6 us -> 23.2 us  [sum_children(): values.reshape(shape[:-3] + (shape[-3] // 2, 2, shape[-2] // 2, 2, shape[...]
  transfers between devices with their start and end apart: 21 -> 22, of which waited for: 12 -> 12; matrix products, arithmetic and copies ran while one was open for 6% -> 5% of each run, Pallas kernels for 0% -> 0%
where the time goes in v1:
time: 412 us; the launch traced here: 407 us
  waiting for transfers between devices  111 us (27%)
  other arithmetic  109 us (26%)
  starting transfers between devices  73.8 us (18%)
  local copies, waits for them, and re-layouts  49.6 us (12%)
  blocking collectives  46 us (11%)
  between operations  15 us (4%)
    add x71, other arithmetic, sweep(): return values + coefs[7] * (right - apply_op(values, pad_z(values), coefs))  81.9 us
    psum x1, waiting for transfers between devices, from_root(): return lax.psum(jnp.where(mine, x, jnp.zeros_like(x)), axis)  65.1 us
    all_gather x1, blocking collectives, spread_cycle(): lax.all_gather(right_side, 'dom', axis=1, tiled=True)  46 us
    ppermute x10, waiting for transfers between devices, padded_2(): after = lax.ppermute(initial, axis, down)  45.3 us
    ppermute x10, starting transfers between devices, padded_2(): before = lax.ppermute(last, axis, up)  32.5 us
    ppermute x10, starting transfers between devices, padded_2(): after = lax.ppermute(initial, axis, down)  31.2 us
    reshape x3, local copies, waits for them, and re-layouts, sum_children(): values.reshape(shape[:-3] + (shape[-3] // 2, 2, shape[-2] // 2, 2, shape[...  23.2 us
    reduce_sum x8, other arithmetic, sum_children(): return split.sum(axis=(-5, -3, -1))  14.2 us
  transfers between devices with their start and end apart: 22, of which 12 were waited for; matrix products, arithmetic and copies ran while one was open for 5% of the time, Pallas kernels for 0%

profile of v1, /device:TPU:120, one launch (start us, length us, event | category | flops | bytes accessed | tf_op | source)
XLA Modules:
  0.0 406.6 jit_solution(666236880155346609)
XLA Ops:
  11.1 65.1 %all-reduce.61.cloned.1.call-done = f32[4,64,128]{1,2,0:T(8,128)} async-done(((f32[4,64,128]{1,2,0:T(8,128)}), f32[4,64,128]{1,2,0:T(8,128)}) %all-reduce.61.cloned.1.call-update) | async-done | bytes 131088 | tf_op jit(solution)/shard_map/psum | solution.py:31
  77.7 9.8 %reshape.764 = f32[2,2,32,2,64,2]{5,4,3,2,1,0:T(8,128)} reshape(f32[1,4,64,128]{3,2,1,0:T(8,128)S(1)} %copy.28) | data formatting | bytes 262144 | tf_op jit(solution)/shard_map/reshape | solution.py:92
  87.5 4.0 reduce_sum.74
  91.8 4.6 %collective-permute-start = (f32[1,1,64,128]{2,3,1,0:T(8,128)S(1)}, f32[1,1,64,128]{2,3,1,0:T(8,128)S(1)}, u32[]{:S(2)}, u32[]{:S(2)}) collective-permute-start(f32[1,1,64,128]{2,3,1,0:T(8,128)S(1)} %get-tuple-element.240), channel_id=1, source_target_pairs={{0,1},{1,2},{2,3},{3,4},{4,5},{5,6},{6,7},{7,8},{8,9},{9,10},{10,1... | collective-permute-start | bytes 98312 | tf_op jit(solution)/shard_map/ppermute | solution.py:23
  96.4 1.9 collective-permute-start.1
  98.3 7.2 %collective-permute-start.4 = (f32[1,1,32,64]{3,2,1,0:T(8,128)S(1)}, f32[1,1,32,64]{3,2,1,0:T(8,128)S(1)}, u32[]{:S(2)}, u32[]{:S(2)}) collective-permute-start(f32[1,1,32,64]{3,2,1,0:T(8,128)S(1)} %get-tuple-element.276), channel_id=1, source_target_pairs={{0,1},{1,2},{2,3},{3,4},{4,5},{5,6},{6,7},{7,8},{8,9},{9,10},{10,1... | collective-permute-start | bytes 24584 | tf_op jit(solution)/shard_map/ppermute | solution.py:23
  105.6 1.9 collective-permute-start.5
  109.0 10.1 %all-to-all-start = ((f32[32,1,512]{2,1,0:T(1,128)}), f32[32,1,512]{2,1,0:T(1,128)}, u32[]{:S(2)}, u32[]{:S(2)}) async-start(f32[32,1,512]{2,1,0:T(1,128)} %reshape.769), calls=%async_computation | async-start | bytes 131072 | tf_op jit(solution)/shard_map/all_to_all | solution.py:153
  119.6 4.6 %collective-permute-start.2 = (f32[1,1,64,128]{2,3,1,0:T(8,128)S(1)}, f32[1,1,64,128]{2,3,1,0:T(8,128)S(1)}, u32[]{:S(2)}, u32[]{:S(2)}) collective-permute-start(f32[1,1,64,128]{2,3,1,0:T(8,128)S(1)} %get-tuple-element.235), channel_id=1, source_target_pairs={{0,1},{1,2},{2,3},{3,4},{4,5},{5,6},{6,7},{7,8},{8,9},{9,10},{10,1... | collective-permute-start | bytes 98312 | tf_op jit(solution)/shard_map/ppermute | solution.py:23
  124.2 1.9 collective-permute-start.3
  126.2 7.5 %collective-permute-done.3 = f32[1,1,64,128]{2,3,1,0:T(8,128)S(1)} collective-permute-done((f32[1,1,64,128]{2,3,1,0:T(8,128)S(1)}, f32[1,1,64,128]{2,3,1,0:T(8,128)S(1)}, u32[]{:S(2)}, u32[]{:S(2)}) %collective-permute-start.3) | collective-permute-done | bytes 32800 | tf_op jit(solution)/shard_map/ppermute | solution.py:24
  134.3 1.9 collective-permute-start.6
  136.2 3.9 collective-permute-start.7
  140.4 5.2 %collective-permute-done.7 = f32[1,1,64,128]{2,3,1,0:T(8,128)S(1)} collective-permute-done((f32[1,1,64,128]{2,3,1,0:T(8,128)S(1)}, f32[1,1,64,128]{2,3,1,0:T(8,128)S(1)}, u32[]{:S(2)}, u32[]{:S(2)}) %collective-permute-start.7) | collective-permute-done | bytes 32800 | tf_op jit(solution)/shard_map/ppermute | solution.py:24
  146.2 9.8 %reshape.765 = f32[2,2,32,2,64,2]{5,4,3,2,1,0:T(8,128)} reshape(f32[1,4,64,128]{3,2,1,0:T(8,128)S(1)} %copy.29) | data formatting | bytes 262144 | tf_op jit(solution)/shard_map/reshape | solution.py:92
  156.0 4.0 reduce_sum.75
  160.2 1.9 collective-permute-start.8
  162.1 3.9 collective-permute-start.9
  166.2 4.9 %collective-permute-done.9 = f32[1,1,32,64]{3,2,1,0:T(8,128)S(1)} collective-permute-done((f32[1,1,32,64]{3,2,1,0:T(8,128)S(1)}, f32[1,1,32,64]{3,2,1,0:T(8,128)S(1)}, u32[]{:S(2)}, u32[]{:S(2)}) %collective-permute-start.9) | collective-permute-done | bytes 8224 | tf_op jit(solution)/shard_map/ppermute | solution.py:24
  171.2 1.9 collective-permute-start.10
  173.1 3.9 collective-permute-start.11
  177.2 4.9 %collective-permute-done.11 = f32[1,1,32,64]{3,2,1,0:T(8,128)S(1)} collective-permute-done((f32[1,1,32,64]{3,2,1,0:T(8,128)S(1)}, f32[1,1,32,64]{3,2,1,0:T(8,128)S(1)}, u32[]{:S(2)}, u32[]{:S(2)}) %collective-permute-start.11) | collective-permute-done | bytes 8224 | tf_op jit(solution)/shard_map/ppermute | solution.py:24
  182.9 46.0 %all-gather = f32[512,32]{1,0:T(8,128)S(1)} all-gather(f32[16,32]{1,0:T(8,128)S(1)} %reduce_sum.82), channel_id=2, replica_groups=mesh['prop'=8,'dom'=32] {'dom'}, dimensions={0}, use_global_device_ids=true | all-gather | bytes 67584 | tf_op jit(solution)/shard_map/all_gather | solution.py:162
  229.4 1.6 reduce.12
  234.5 3.6 reshape_reshape.3
  238.1 2.5 reduce_sum.84
  243.3 1.6 fusion.17
  245.0 3.6 reshape.767
  248.6 3.2 reduce_sum.85
  251.8 1.9 broadcast_divide_fusion
  254.6 84.1 %while.15 = (s32[]{:T(128)}, f32[1,16,8,16]{3,2,1,0:T(8,128)S(1)}, f32[1,16,8,16]{3,2,1,0:T(8,128)}, f32[1,16,8,16]{3,2,1,0:T(8,128)}, f32[1,16,8,16]{3,2,1,0:T(...) while((s32[]{:T(128)}, f32[1,16,8,16]{3,2,1,0:T(8,128)S(1)}, ...), condition=%wide.region_10.11_spmd, body=%wide.region_9.10_spmd.sunk | while | flops 32770 | bytes 195701 | solution.py:116
  254.7 1.2 fusion.159
  256.0 1.2 fusion.159
  257.4 1.2 fusion.159
  260.0 1.2 fusion.159
  274.7 1.2 fusion.159
  277.4 1.2 fusion.159
  280.1 1.2 fusion.159
  282.7 1.2 fusion.159
  285.4 1.2 fusion.159
  300.1 1.2 fusion.159
  302.7 1.2 fusion.159
  305.4 1.2 fusion.159
  308.1 1.2 fusion.159
  310.7 1.2 fusion.159
  325.4 1.2 fusion.159
  328.1 1.2 fusion.159
  330.8 1.2 fusion.159
  333.4 1.2 fusion.159
  336.1 1.2 fusion.159
  341.1 1.8 copy.31
  344.2 1.3 fusion.24
  346.9 4.6 %collective-permute-start.12 = (f32[1,1,32,64]{3,2,1,0:T(8,128)S(1)}, f32[1,1,32,64]{3,2,1,0:T(8,128)S(1)}, u32[]{:S(2)}, u32[]{:S(2)}) collective-permute-start(f32[1,1,32,64]{3,2,1,0:T(8,128)S(1)} %get-tuple-element.257), channel_id=1, source_target_pairs={{0,1},{1,2},{2,3},{3,4},{4,5},{5,6},{6,7},{7,8},{8,9},{9,10},{10,1... | collective-permute-start | bytes 24584 | tf_op jit(solution)/shard_map/ppermute | solution.py:23
  351.5 1.9 collective-permute-start.13
  353.5 7.1 %collective-permute-done.13 = f32[1,1,32,64]{3,2,1,0:T(8,128)S(1)} collective-permute-done((f32[1,1,32,64]{3,2,1,0:T(8,128)S(1)}, f32[1,1,32,64]{3,2,1,0:T(8,128)S(1)}, u32[]{:S(2)}, u32[]{:S(2)}) %collective-permute-start.13) | collective-permute-done | bytes 8224 | tf_op jit(solution)/shard_map/ppermute | solution.py:24
  361.5 1.9 collective-permute-start.14
  363.5 3.9 collective-permute-start.15
  367.5 5.0 %collective-permute-done.15 = f32[1,1,32,64]{3,2,1,0:T(8,128)S(1)} collective-permute-done((f32[1,1,32,64]{3,2,1,0:T(8,128)S(1)}, f32[1,1,32,64]{3,2,1,0:T(8,128)S(1)}, u32[]{:S(2)}, u32[]{:S(2)}) %collective-permute-start.15) | collective-permute-done | bytes 8224 | tf_op jit(solution)/shard_map/ppermute | solution.py:24
  373.8 1.9 collective-permute-start.16
  375.7 3.9 collective-permute-start.17
  380.0 5.2 %collective-permute-done.17 = f32[1,1,64,128]{2,3,1,0:T(8,128)S(1)} collective-permute-done((f32[1,1,64,128]{2,3,1,0:T(8,128)S(1)}, f32[1,1,64,128]{2,3,1,0:T(8,128)S(1)}, u32[]{:S(2)}, u32[]{:S(2)}) %collective-permute-start.17) | collective-permute-done | bytes 32800 | tf_op jit(solution)/shard_map/ppermute | solution.py:24
  386.5 1.9 collective-permute-start.18
  388.4 3.9 collective-permute-start.19
  392.6 5.2 %collective-permute-done.19 = f32[1,1,64,128]{2,3,1,0:T(8,128)S(1)} collective-permute-done((f32[1,1,64,128]{2,3,1,0:T(8,128)S(1)}, f32[1,1,64,128]{2,3,1,0:T(8,128)S(1)}, u32[]{:S(2)}, u32[]{:S(2)}) %collective-permute-start.19) | collective-permute-done | bytes 32800 | tf_op jit(solution)/shard_map/ppermute | solution.py:24
  (395 shorter events, 87.6 us)
Async XLA Ops:
  6.5 69.6 %all-reduce.61.cloned.1.call-start = ((), (), s32[]{:S(2)}) async-start(), calls=%async_computation.1 | async-start | bytes 524288 | tf_op jit(solution)/shard_map/psum | solution.py:31
  77.2 68.5 %copy-start.20 = (f32[1,4,64,1]{2,3,1,0:T(1,128)}, f32[1,4,64,1]{2,3,1,0:T(1,128)S(1)}, u32[]{:S(2)}) copy-start(f32[1,4,64,1]{2,3,1,0:T(1,128)S(1)} %get-tuple-element.241) | copy-start | bytes 3076
  77.2 68.5 %copy-start.21 = (f32[1,4,64,1]{2,3,1,0:T(1,128)}, f32[1,4,64,1]{2,3,1,0:T(1,128)S(1)}, u32[]{:S(2)}) copy-start(f32[1,4,64,1]{2,3,1,0:T(1,128)S(1)} %get-tuple-element.242) | copy-start | bytes 3076
  91.5 90.6 %copy-start.22 = (f32[1,2,1,64]{3,2,1,0:T(1,128)}, f32[1,2,1,64]{3,2,1,0:T(1,128)S(1)}, u32[]{:S(2)}) copy-start(f32[1,2,1,64]{3,2,1,0:T(1,128)S(1)} %get-tuple-element.277) | copy-start | bytes 1540
  91.5 90.6 %copy-start.23 = (f32[1,2,1,64]{3,2,1,0:T(1,128)}, f32[1,2,1,64]{3,2,1,0:T(1,128)S(1)}, u32[]{:S(2)}) copy-start(f32[1,2,1,64]{3,2,1,0:T(1,128)S(1)} %get-tuple-element.278) | copy-start | bytes 1540
  91.6 90.5 %copy-start.10 = (f32[1,2,31,64]{3,2,1,0:T(8,128)}, f32[1,2,31,64]{3,2,1,0:T(8,128)S(1)}, u32[]{:S(2)}) copy-start(f32[1,2,31,64]{3,2,1,0:T(8,128)S(1)} %add_divide_fusion.7) | copy-start | bytes 47620
  91.8 27.3 %collective-permute-start = (f32[1,1,64,128]{2,3,1,0:T(8,128)S(1)}, f32[1,1,64,128]{2,3,1,0:T(8,128)S(1)}, u32[]{:S(2)}, u32[]{:S(2)}) collective-permute-start(f32[1,1,64,128]{2,3,1,0:T(8,128)S(1)} %get-tuple-element.240), channel_id=1, source_target_pairs={{0,1},{1,2},{2,3},{3,4},{4,5},{5,6},{6,7},{7,8},{8,9},{9,10},{10,1... | collective-permute-start | bytes 98312 | tf_op jit(solution)/shard_map/ppermute | solution.py:23
  96.4 22.7 %collective-permute-start.1 = (f32[1,1,64,128]{2,3,1,0:T(8,128)S(1)}, f32[1,1,64,128]{2,3,1,0:T(8,128)S(1)}, u32[]{:S(2)}, u32[]{:S(2)}) collective-permute-start(f32[1,1,64,128]{2,3,1,0:T(8,128)S(1)} %get-tuple-element.239), channel_id=1, source_target_pairs={{1,0},{2,1},{3,2},{4,3},{5,4},{6,5},{7,6},{8,7},{9,8},{10,9},{11,1... | collective-permute-start | bytes 98312 | tf_op jit(solution)/shard_map/ppermute | solution.py:24
  98.3 61.7 %collective-permute-start.4 = (f32[1,1,32,64]{3,2,1,0:T(8,128)S(1)}, f32[1,1,32,64]{3,2,1,0:T(8,128)S(1)}, u32[]{:S(2)}, u32[]{:S(2)}) collective-permute-start(f32[1,1,32,64]{3,2,1,0:T(8,128)S(1)} %get-tuple-element.276), channel_id=1, source_target_pairs={{0,1},{1,2},{2,3},{3,4},{4,5},{5,6},{6,7},{7,8},{8,9},{9,10},{10,1... | collective-permute-start | bytes 24584 | tf_op jit(solution)/shard_map/ppermute | solution.py:23
  105.6 54.5 %collective-permute-start.5 = (f32[1,1,32,64]{3,2,1,0:T(8,128)S(1)}, f32[1,1,32,64]{3,2,1,0:T(8,128)S(1)}, u32[]{:S(2)}, u32[]{:S(2)}) collective-permute-start(f32[1,1,32,64]{3,2,1,0:T(8,128)S(1)} %get-tuple-element.275), channel_id=1, source_target_pairs={{1,0},{2,1},{3,2},{4,3},{5,4},{6,5},{7,6},{8,7},{9,8},{10,9},{11,1... | collective-permute-start | bytes 24584 | tf_op jit(solution)/shard_map/ppermute | solution.py:24
  109.0 119.9 %all-to-all-start = ((f32[32,1,512]{2,1,0:T(1,128)}), f32[32,1,512]{2,1,0:T(1,128)}, u32[]{:S(2)}, u32[]{:S(2)}) async-start(f32[32,1,512]{2,1,0:T(1,128)} %reshape.769), calls=%async_computation | async-start | bytes 131072 | tf_op jit(solution)/shard_map/all_to_all | solution.py:153
  119.1 36.9 %copy-start.4 = (f32[1,1,64,128]{2,3,1,0:T(8,128)}, f32[1,1,64,128]{2,3,1,0:T(8,128)S(1)}, u32[]{:S(2)}) copy-start(f32[1,1,64,128]{2,3,1,0:T(8,128)S(1)} %collective-permute-done) | copy-start | bytes 98308
  119.1 36.9 %copy-start.6 = (f32[1,1,64,128]{2,3,1,0:T(8,128)}, f32[1,1,64,128]{2,3,1,0:T(8,128)S(1)}, u32[]{:S(2)}) copy-start(f32[1,1,64,128]{2,3,1,0:T(8,128)S(1)} %collective-permute-done.1) | copy-start | bytes 98308
  119.6 6.6 %collective-permute-start.2 = (f32[1,1,64,128]{2,3,1,0:T(8,128)S(1)}, f32[1,1,64,128]{2,3,1,0:T(8,128)S(1)}, u32[]{:S(2)}, u32[]{:S(2)}) collective-permute-start(f32[1,1,64,128]{2,3,1,0:T(8,128)S(1)} %get-tuple-element.235), channel_id=1, source_target_pairs={{0,1},{1,2},{2,3},{3,4},{4,5},{5,6},{6,7},{7,8},{8,9},{9,10},{10,1... | collective-permute-start | bytes 98312 | tf_op jit(solution)/shard_map/ppermute | solution.py:23
  124.2 9.5 %collective-permute-start.3 = (f32[1,1,64,128]{2,3,1,0:T(8,128)S(1)}, f32[1,1,64,128]{2,3,1,0:T(8,128)S(1)}, u32[]{:S(2)}, u32[]{:S(2)}) collective-permute-start(f32[1,1,64,128]{2,3,1,0:T(8,128)S(1)} %get-tuple-element.236), channel_id=1, source_target_pairs={{1,0},{2,1},{3,2},{4,3},{5,4},{6,5},{7,6},{8,7},{9,8},{10,9},{11,1... | collective-permute-start | bytes 98312 | tf_op jit(solution)/shard_map/ppermute | solution.py:24
  134.3 6.2 %collective-permute-start.6 = (f32[1,1,64,128]{2,3,1,0:T(8,128)S(1)}, f32[1,1,64,128]{2,3,1,0:T(8,128)S(1)}, u32[]{:S(2)}, u32[]{:S(2)}) collective-permute-start(f32[1,1,64,128]{2,3,1,0:T(8,128)S(1)} %get-tuple-element.229), channel_id=1, source_target_pairs={{0,1},{1,2},{2,3},{3,4},{4,5},{5,6},{6,7},{7,8},{8,9},{9,10},{10,1... | collective-permute-start | bytes 98312 | tf_op jit(solution)/shard_map/ppermute | solution.py:23
  136.2 9.5 %collective-permute-start.7 = (f32[1,1,64,128]{2,3,1,0:T(8,128)S(1)}, f32[1,1,64,128]{2,3,1,0:T(8,128)S(1)}, u32[]{:S(2)}, u32[]{:S(2)}) collective-permute-start(f32[1,1,64,128]{2,3,1,0:T(8,128)S(1)} %get-tuple-element.230), channel_id=1, source_target_pairs={{1,0},{2,1},{3,2},{4,3},{5,4},{6,5},{7,6},{8,7},{9,8},{10,9},{11,1... | collective-permute-start | bytes 98312 | tf_op jit(solution)/shard_map/ppermute | solution.py:24
  160.0 74.5 %copy-start.8 = (f32[2,32,64]{2,1,0:T(8,128)}, f32[2,32,64]{2,1,0:T(8,128)S(1)}, u32[]{:S(2)}) copy-start(f32[2,32,64]{2,1,0:T(8,128)S(1)} %reduce_sum.75) | copy-start | bytes 49156
  160.0 71.3 %copy-start.18 = (f32[1,1,32,64]{3,2,1,0:T(8,128)}, f32[1,1,32,64]{3,2,1,0:T(8,128)S(1)}, u32[]{:S(2)}) copy-start(f32[1,1,32,64]{3,2,1,0:T(8,128)S(1)} %collective-permute-done.4) | copy-start | bytes 24580
  160.0 71.3 %copy-start.19 = (f32[1,1,32,64]{3,2,1,0:T(8,128)}, f32[1,1,32,64]{3,2,1,0:T(8,128)S(1)}, u32[]{:S(2)}) copy-start(f32[1,1,32,64]{3,2,1,0:T(8,128)S(1)} %collective-permute-done.5) | copy-start | bytes 24580
  160.2 71.2 %copy-start.12 = (f32[1,2,32,64]{3,2,1,0:T(8,128)}, f32[1,2,32,64]{3,2,1,0:T(8,128)S(1)}, u32[]{:S(2)}) copy-start(f32[1,2,32,64]{3,2,1,0:T(8,128)S(1)} %get-tuple-element.180) | copy-start | bytes 49156
  160.2 71.2 %copy-start.14 = (f32[1,2,32,64]{3,2,1,0:T(8,128)}, f32[1,2,32,64]{3,2,1,0:T(8,128)S(1)}, u32[]{:S(2)}) copy-start(f32[1,2,32,64]{3,2,1,0:T(8,128)S(1)} %get-tuple-element.181) | copy-start | bytes 49156
  160.2 5.9 %collective-permute-start.8 = (f32[1,1,32,64]{3,2,1,0:T(8,128)S(1)}, f32[1,1,32,64]{3,2,1,0:T(8,128)S(1)}, u32[]{:S(2)}, u32[]{:S(2)}) collective-permute-start(f32[1,1,32,64]{3,2,1,0:T(8,128)S(1)} %get-tuple-element.271), channel_id=1, source_target_pairs={{0,1},{1,2},{2,3},{3,4},{4,5},{5,6},{6,7},{7,8},{8,9},{9,10},{10,1... | collective-permute-start | bytes 24584 | tf_op jit(solution)/shard_map/ppermute | solution.py:23
  162.1 9.0 %collective-permute-start.9 = (f32[1,1,32,64]{3,2,1,0:T(8,128)S(1)}, f32[1,1,32,64]{3,2,1,0:T(8,128)S(1)}, u32[]{:S(2)}, u32[]{:S(2)}) collective-permute-start(f32[1,1,32,64]{3,2,1,0:T(8,128)S(1)} %get-tuple-element.272), channel_id=1, source_target_pairs={{1,0},{2,1},{3,2},{4,3},{5,4},{6,5},{7,6},{8,7},{9,8},{10,9},{11,1... | collective-permute-start | bytes 24584 | tf_op jit(solution)/shard_map/ppermute | solution.py:24
  171.2 5.9 %collective-permute-start.10 = (f32[1,1,32,64]{3,2,1,0:T(8,128)S(1)}, f32[1,1,32,64]{3,2,1,0:T(8,128)S(1)}, u32[]{:S(2)}, u32[]{:S(2)}) collective-permute-start(f32[1,1,32,64]{3,2,1,0:T(8,128)S(1)} %get-tuple-element.265), channel_id=1, source_target_pairs={{0,1},{1,2},{2,3},{3,4},{4,5},{5,6},{6,7},{7,8},{8,9},{9,10},{10,1... | collective-permute-start | bytes 24584 | tf_op jit(solution)/shard_map/ppermute | solution.py:23
  173.1 9.0 %collective-permute-start.11 = (f32[1,1,32,64]{3,2,1,0:T(8,128)S(1)}, f32[1,1,32,64]{3,2,1,0:T(8,128)S(1)}, u32[]{:S(2)}, u32[]{:S(2)}) collective-permute-start(f32[1,1,32,64]{3,2,1,0:T(8,128)S(1)} %get-tuple-element.266), channel_id=1, source_target_pairs={{1,0},{2,1},{3,2},{4,3},{5,4},{6,5},{7,6},{8,7},{9,8},{10,9},{11,1... | collective-permute-start | bytes 24584 | tf_op jit(solution)/shard_map/ppermute | solution.py:24
  231.2 6.9 %copy-start.16 = (f32[1,32,1,32]{3,2,1,0:T(1,128)}, f32[1,32,1,32]{3,2,1,0:T(1,128)S(1)}, u32[]{:S(2)}) copy-start(f32[1,32,1,32]{3,2,1,0:T(1,128)S(1)} %get-tuple-element.224) | copy-start | bytes 12292
  232.0 0.7 copy-start
  232.0 1.6 copy-start.3
  248.6 95.6 %copy-start.1 = (f32[1,32,16,32]{3,2,1,0:T(8,128)S(1)}, f32[1,32,16,32]{3,2,1,0:T(8,128)}, u32[]{:S(2)}) copy-start(f32[1,32,16,32]{3,2,1,0:T(8,128)} %copy-done) | copy-start | bytes 196612
  253.7 0.9 copy-start.2
  342.9 2.8 copy-start.17
  343.9 16.7 %copy-start.9 = (f32[2,32,64]{2,1,0:T(8,128)S(1)}, f32[2,32,64]{2,1,0:T(8,128)}, u32[]{:S(2)}) copy-start(f32[2,32,64]{2,1,0:T(8,128)} %copy-done.8) | copy-start | bytes 49156
  343.9 16.7 %copy-start.11 = (f32[1,2,31,64]{3,2,1,0:T(8,128)S(1)}, f32[1,2,31,64]{3,2,1,0:T(8,128)}, u32[]{:S(2)}) copy-start(f32[1,2,31,64]{3,2,1,0:T(8,128)} %copy-done.10) | copy-start | bytes 47620
  343.9 16.7 %copy-start.13 = (f32[1,2,32,64]{3,2,1,0:T(8,128)S(1)}, f32[1,2,32,64]{3,2,1,0:T(8,128)}, u32[]{:S(2)}) copy-start(f32[1,2,32,64]{3,2,1,0:T(8,128)} %copy-done.12) | copy-start | bytes 49156
  343.9 16.7 %copy-start.15 = (f32[1,2,32,64]{3,2,1,0:T(8,128)S(1)}, f32[1,2,32,64]{3,2,1,0:T(8,128)}, u32[]{:S(2)}) copy-start(f32[1,2,32,64]{3,2,1,0:T(8,128)} %copy-done.14) | copy-start | bytes 49156
  344.0 41.2 %copy-start.5 = (f32[1,1,64,128]{2,3,1,0:T(8,128)S(1)}, f32[1,1,64,128]{2,3,1,0:T(8,128)}, u32[]{:S(2)}) copy-start(f32[1,1,64,128]{2,3,1,0:T(8,128)} %copy-done.4) | copy-start | bytes 98308
  344.0 41.2 %copy-start.7 = (f32[1,1,64,128]{2,3,1,0:T(8,128)S(1)}, f32[1,1,64,128]{2,3,1,0:T(8,128)}, u32[]{:S(2)}) copy-start(f32[1,1,64,128]{2,3,1,0:T(8,128)} %copy-done.6) | copy-start | bytes 98308
  346.9 6.6 %collective-permute-start.12 = (f32[1,1,32,64]{3,2,1,0:T(8,128)S(1)}, f32[1,1,32,64]{3,2,1,0:T(8,128)S(1)}, u32[]{:S(2)}, u32[]{:S(2)}) collective-permute-start(f32[1,1,32,64]{3,2,1,0:T(8,128)S(1)} %get-tuple-element.257), channel_id=1, source_target_pairs={{0,1},{1,2},{2,3},{3,4},{4,5},{5,6},{6,7},{7,8},{8,9},{9,10},{10,1... | collective-permute-start | bytes 24584 | tf_op jit(solution)/shard_map/ppermute | solution.py:23
  351.5 9.1 %collective-permute-start.13 = (f32[1,1,32,64]{3,2,1,0:T(8,128)S(1)}, f32[1,1,32,64]{3,2,1,0:T(8,128)S(1)}, u32[]{:S(2)}, u32[]{:S(2)}) collective-permute-start(f32[1,1,32,64]{3,2,1,0:T(8,128)S(1)} %get-tuple-element.258), channel_id=1, source_target_pairs={{1,0},{2,1},{3,2},{4,3},{5,4},{6,5},{7,6},{8,7},{9,8},{10,9},{11,1... | collective-permute-start | bytes 24584 | tf_op jit(solution)/shard_map/ppermute | solution.py:24
  361.5 5.9 %collective-permute-start.14 = (f32[1,1,32,64]{3,2,1,0:T(8,128)S(1)}, f32[1,1,32,64]{3,2,1,0:T(8,128)S(1)}, u32[]{:S(2)}, u32[]{:S(2)}) collective-permute-start(f32[1,1,32,64]{3,2,1,0:T(8,128)S(1)} %get-tuple-element.251), channel_id=1, source_target_pairs={{0,1},{1,2},{2,3},{3,4},{4,5},{5,6},{6,7},{7,8},{8,9},{9,10},{10,1... | collective-permute-start | bytes 24584 | tf_op jit(solution)/shard_map/ppermute | solution.py:23
  363.5 9.0 %collective-permute-start.15 = (f32[1,1,32,64]{3,2,1,0:T(8,128)S(1)}, f32[1,1,32,64]{3,2,1,0:T(8,128)S(1)}, u32[]{:S(2)}, u32[]{:S(2)}) collective-permute-start(f32[1,1,32,64]{3,2,1,0:T(8,128)S(1)} %get-tuple-element.252), channel_id=1, source_target_pairs={{1,0},{2,1},{3,2},{4,3},{5,4},{6,5},{7,6},{8,7},{9,8},{10,9},{11,1... | collective-permute-start | bytes 24584 | tf_op jit(solution)/shard_map/ppermute | solution.py:24
  373.8 6.2 %collective-permute-start.16 = (f32[1,1,64,128]{2,3,1,0:T(8,128)S(1)}, f32[1,1,64,128]{2,3,1,0:T(8,128)S(1)}, u32[]{:S(2)}, u32[]{:S(2)}) collective-permute-start(f32[1,1,64,128]{2,3,1,0:T(8,128)S(1)} %get-tuple-element.199), channel_id=1, source_target_pairs={{0,1},{1,2},{2,3},{3,4},{4,5},{5,6},{6,7},{7,8},{8,9},{9,10},{10,1... | collective-permute-start | bytes 98312 | tf_op jit(solution)/shard_map/ppermute | solution.py:23
  375.7 9.5 %collective-permute-start.17 = (f32[1,1,64,128]{2,3,1,0:T(8,128)S(1)}, f32[1,1,64,128]{2,3,1,0:T(8,128)S(1)}, u32[]{:S(2)}, u32[]{:S(2)}) collective-permute-start(f32[1,1,64,128]{2,3,1,0:T(8,128)S(1)} %get-tuple-element.200), channel_id=1, source_target_pairs={{1,0},{2,1},{3,2},{4,3},{5,4},{6,5},{7,6},{8,7},{9,8},{10,9},{11,1... | collective-permute-start | bytes 98312 | tf_op jit(solution)/shard_map/ppermute | solution.py:24
  386.5 6.2 %collective-permute-start.18 = (f32[1,1,64,128]{2,3,1,0:T(8,128)S(1)}, f32[1,1,64,128]{2,3,1,0:T(8,128)S(1)}, u32[]{:S(2)}, u32[]{:S(2)}) collective-permute-start(f32[1,1,64,128]{2,3,1,0:T(8,128)S(1)} %get-tuple-element.193), channel_id=1, source_target_pairs={{0,1},{1,2},{2,3},{3,4},{4,5},{5,6},{6,7},{7,8},{8,9},{9,10},{10,1... | collective-permute-start | bytes 98312 | tf_op jit(solution)/shard_map/ppermute | solution.py:23
  388.4 9.5 %collective-permute-start.19 = (f32[1,1,64,128]{2,3,1,0:T(8,128)S(1)}, f32[1,1,64,128]{2,3,1,0:T(8,128)S(1)}, u32[]{:S(2)}, u32[]{:S(2)}) collective-permute-start(f32[1,1,64,128]{2,3,1,0:T(8,128)S(1)} %get-tuple-element.194), channel_id=1, source_target_pairs={{1,0},{2,1},{3,2},{4,3},{5,4},{6,5},{7,6},{8,7},{9,8},{10,9},{11,1... | collective-permute-start | bytes 98312 | tf_op jit(solution)/shard_map/ppermute | solution.py:24
Sparse Core Ops, SparseCore 0:
  9.7 66.4 all-reduce.60
